TPU v7x, 32 devices: a whole 2x2x4 slice. The times are simulated.
32 devices in a mesh: pts: 8 (over z, y), grp: 4 (over x, core).
Axes of the slice: x: 2, y: 2, z: 4, core: 2. Of those that a mesh axis runs over, the one named last changes fastest.
Arguments:
- jacobian: bfloat16 [32, 6, 128, 3, 256], P(('pts', 'grp')), may hold values from -0.21875 to 0.21875
- point_blocks: float32 [32, 6, 256], P(('pts', 'grp')), may hold values from -0.5 to 4, as said below
- point_grad: bfloat16 [32, 3, 256], P(('pts', 'grp')), may hold values from -6 to 6
- camera_grad: float32 [32, 128], P(('pts', 'grp')), may hold values from -6 to 6
- damping: float32 [32, 128], replicated, may hold values from 1 to 8
- incidence: int32 [32, 6], P(('pts', 'grp')), may hold values from 0 to 31, as said below
- tile_owner: int32 [8], replicated, may hold values from 0 to 7, each once
- front_first: int32 [1], replicated, may hold values from 0 to 31
Outputs:
- tiles_out: float32 [256, 128, 128], P(('pts', 'grp'))
- rhs_out: float32 [32, 128], P(('pts', 'grp'))
- front_panel: float32 [2304, 512], P(None, 'grp')
Inputs may be any that keep to these rules, and one draw needn't show every extreme that they name: `incidence`: point cluster p names 6 different camera clusters, all among (p + t) mod 32 for t from 0 to 7. `point_blocks`: each point's diagonal entries exceed the sum of the magnitudes of the two off-diagonal entries of their row by 0.1 or more. `tile_owner`: A permutation of the pts indices.
All inputs are finite; a program needn't handle non-finite values.
Results may differ from a plain program's by a relative error of at most 0.0022.
Values sent between devices are 32-bit elements; how exact they have to be, the bound alone decides.
No kernel may reach another device: no remote copies, remote signals or barrier semaphores. Data moves between devices by JAX's collectives and lax.ppermute only.
A program may use at most 128 MiB of HBM per device.

v0:
```python
import jax
import jax.numpy as jnp
import numpy as np
from jax import lax
from jax.sharding import PartitionSpec as P

TOUCH = 6
BAND = 8
FRONT = 4
PRECISE = lax.Precision.HIGHEST


def shifted(value, axis, steps):
    count = lax.axis_size(axis)
    pairs = [(source, (source + steps) % count) for source in range(count)]
    return lax.ppermute(value, axis, pairs)


def invert_blocks(blocks):
    diag_x = blocks[:, 0]
    diag_y = blocks[:, 1]
    diag_z = blocks[:, 2]
    cross_xy = blocks[:, 3]
    cross_xz = blocks[:, 4]
    cross_yz = blocks[:, 5]
    adj_xx = diag_y * diag_z - cross_yz * cross_yz
    adj_yy = diag_x * diag_z - cross_xz * cross_xz
    adj_zz = diag_x * diag_y - cross_xy * cross_xy
    adj_xy = cross_xz * cross_yz - cross_xy * diag_z
    adj_xz = cross_xy * cross_yz - diag_y * cross_xz
    adj_yz = cross_xy * cross_xz - diag_x * cross_yz
    determinant = diag_x * adj_xx + cross_xy * adj_xy + cross_xz * adj_xz
    inverse_det = 1.0 / determinant
    return [
        [adj_xx * inverse_det, adj_xy * inverse_det, adj_xz * inverse_det],
        [adj_xy * inverse_det, adj_yy * inverse_det, adj_yz * inverse_det],
        [adj_xz * inverse_det, adj_yz * inverse_det, adj_zz * inverse_det],
    ]


def scale_jacobian(jacobian, blocks):
    inverse = invert_blocks(blocks)
    widened = jacobian.astype(jnp.float32)
    columns = []
    for target in range(3):
        summed = widened[:, :, :, 0, :] * inverse[0][target][:, None, None, :]
        summed = summed + widened[:, :, :, 1, :] * inverse[1][target][:, None, None, :]
        summed = summed + widened[:, :, :, 2, :] * inverse[2][target][:, None, None, :]
        columns.append(summed)
    return jnp.stack(columns, axis=3).astype(jnp.bfloat16)


def band_table(reach_rows, reach_sum):
    row_list = []
    offset_list = []
    for row_pos in range(reach_rows):
        for offset in range(BAND):
            if row_pos + offset <= reach_sum:
                row_list.append(row_pos)
                offset_list.append(offset)
    return (np.array(row_list), np.array(offset_list))


def route_rows(tiles, tile_owner, base, row_list, offset_list, pts_count):
    offsets = BAND * row_list + offset_list
    capacity = int(offsets.max()) // pts_count + 1
    residue = jnp.mod(base + jnp.asarray(offsets), pts_count)
    target = tile_owner[residue] * capacity + jnp.asarray(offsets // pts_count)
    sending = (jnp.arange(pts_count * capacity)[:, None] == target[None, :]).astype(jnp.float32)
    return (jnp.einsum("dt,trc->drc", sending, tiles, precision=PRECISE), capacity)


def collect_rows(
    incoming, capacity, perm_inverse, anchors, usable_test, clusters, grp_count, pts_count
):
    sender = jnp.arange(pts_count * capacity) // capacity
    slot_of = jnp.arange(pts_count * capacity) % capacity
    sender_anchor = anchors(sender)
    arrived = jnp.mod(perm_inverse - BAND * sender_anchor, pts_count) + slot_of * pts_count
    row_pos = arrived // BAND
    offset = arrived % BAND
    usable = usable_test(row_pos, offset)
    home_row = jnp.mod(sender_anchor + row_pos, clusters)
    owner_slot = (BAND * home_row + offset) // pts_count
    gathering = (
        (jnp.arange(BAND * grp_count)[:, None] == owner_slot[None, :]) & usable[None, :]
    ).astype(jnp.float32)
    return jnp.einsum("ms,src->mrc", gathering, incoming, precision=PRECISE)


def per_device(
    jacobian, point_blocks, point_grad, camera_grad, damping, incidence, tile_owner, front_first
):
    pts_count = lax.axis_size("pts")
    grp_count = lax.axis_size("grp")
    clusters = pts_count * grp_count
    my_grp = lax.axis_index("grp")
    my_pts = lax.axis_index("pts")
    device = my_pts * grp_count + my_grp
    local_count = jacobian.shape[0]
    cam_rows = jacobian.shape[2]
    point_cols = 3 * jacobian.shape[4]
    window_len = 2 * BAND - 2 + FRONT
    reach = 2 * BAND - 1
    scaled = scale_jacobian(jacobian, point_blocks).reshape(
        local_count, TOUCH, cam_rows, point_cols
    )
    jac_flat = jacobian.reshape(local_count, TOUCH, cam_rows, point_cols)
    local_slot = jnp.mod(incidence - device, clusters)
    placing = (local_slot[:, None, :] == jnp.arange(BAND)[None, :, None]).astype(jnp.bfloat16)
    placed_scaled = jnp.einsum(
        "ptk,pkrx->ptrx", placing, scaled, preferred_element_type=jnp.float32
    ).astype(jnp.bfloat16)
    placed_jac = jnp.einsum(
        "ptk,pkrx->ptrx", placing, jac_flat, preferred_element_type=jnp.float32
    ).astype(jnp.bfloat16)
    band_grid = jnp.einsum(
        "ptrx,pqcx->tqrc", placed_scaled, placed_jac, preferred_element_type=jnp.float32
    )
    band_rhs = jnp.einsum(
        "ptrx,px->tr",
        placed_scaled,
        point_grad.reshape(local_count, point_cols),
        preferred_element_type=jnp.float32,
    )
    perm_inverse = jnp.sum(jnp.arange(pts_count) * (tile_owner == my_pts))
    row_list, offset_list = band_table(BAND, BAND - 1)
    band_tiles = band_grid[row_list, row_list + offset_list]
    quarters = lax.all_to_all(band_tiles, "grp", split_axis=1, concat_axis=0, tiled=True)
    reach_union = BAND + grp_count - 2
    union_rows_list, union_offsets = band_table(reach_union + 1, reach_union)
    lookup = {}
    for position in range(len(union_rows_list)):
        lookup[int(union_rows_list[position]), int(union_offsets[position])] = position
    merge_table = np.zeros((len(union_rows_list), grp_count * len(row_list)), np.float32)
    for source_grp in range(grp_count):
        for position in range(len(row_list)):
            merge_table[
                lookup[source_grp + int(row_list[position]), int(offset_list[position])],
                source_grp * len(row_list) + position,
            ] = 1.0
    union_rows = jnp.einsum("us,src->urc", jnp.asarray(merge_table), quarters, precision=PRECISE)
    outgoing, capacity = route_rows(
        union_rows, tile_owner, BAND * grp_count * my_pts, union_rows_list, union_offsets, pts_count
    )
    incoming = lax.all_to_all(outgoing, "pts", split_axis=0, concat_axis=0, tiled=True)
    owner_rows = collect_rows(
        incoming,
        capacity,
        perm_inverse,
        lambda sender: sender * grp_count,
        lambda row_pos, offset: row_pos + offset <= reach_union,
        clusters,
        grp_count,
        pts_count,
    )
    owned = lax.all_to_all(owner_rows, "grp", split_axis=0, concat_axis=1, tiled=True)
    tile_id = perm_inverse + pts_count * (BAND * my_grp + jnp.arange(BAND))
    home_row = tile_id // BAND
    offset = tile_id % BAND
    other_row = jnp.mod(home_row + offset, clusters)
    pick_damp = (home_row[:, None] == jnp.arange(clusters)[None, :]).astype(jnp.float32)
    damp_rows = jnp.dot(pick_damp, damping, precision=PRECISE)
    identity = jnp.eye(cam_rows, dtype=jnp.float32)
    owned = owned + jnp.where(
        (offset == 0)[:, None, None], damp_rows[:, :, None] * identity[None, :, :], 0.0
    )
    summed = band_rhs[0]
    for step in range(1, BAND):
        summed = summed + shifted(band_rhs[step], ("pts", "grp"), step)
    reduced = camera_grad - summed[None, :]
    front_start = front_first[0]
    window_base = front_start - (BAND - 1)
    pos_home = jnp.mod(home_row - window_base, clusters)
    pos_other = jnp.mod(other_row - window_base, clusters)
    front_axis = jnp.arange(FRONT)[:, None, None]
    reach_axis = jnp.arange(reach)[None, :, None]
    direct = (
        (pos_other[None, None, :] == BAND - 1 + front_axis)
        & (pos_home[None, None, :] == front_axis + reach_axis)
    ).astype(jnp.float32)
    mirror = (
        (pos_home[None, None, :] == BAND - 1 + front_axis)
        & (offset[None, None, :] > 0)
        & (pos_other[None, None, :] == front_axis + reach_axis)
    ).astype(jnp.float32)
    front_rows = jnp.einsum("kes,sab->keab", direct, owned, precision=PRECISE) + jnp.einsum(
        "kes,sba->keab", mirror, owned, precision=PRECISE
    )
    my_pos = jnp.mod(device - window_base, clusters)
    window_rhs = (jnp.arange(window_len)[:, None] == my_pos).astype(jnp.float32) * reduced
    front_rows, window_rhs = lax.psum((front_rows, window_rhs), ("pts", "grp"))
    flat_rows = jnp.concatenate(
        [
            front_rows.reshape(FRONT * reach, cam_rows, cam_rows),
            jnp.zeros((1, cam_rows, cam_rows), jnp.float32),
        ],
        axis=0,
    )
    lookup_table = np.full((window_len, FRONT), FRONT * reach, np.int32)
    for position in range(window_len):
        for front_pos in range(FRONT):
            if 0 <= position - front_pos < reach:
                lookup_table[position, front_pos] = front_pos * reach + position - front_pos
    columns = (
        flat_rows[lookup_table]
        .transpose(0, 2, 1, 3)
        .reshape(window_len * cam_rows, FRONT * cam_rows)
    )
    square = columns[(BAND - 1) * cam_rows : (BAND - 1 + FRONT) * cam_rows]
    factor = jnp.linalg.cholesky(square)
    panel = jax.scipy.linalg.solve_triangular(factor, columns.T, lower=True).T
    share = FRONT * cam_rows // grp_count
    front_panel = lax.dynamic_slice_in_dim(panel, my_grp * share, share, 1)
    panel_blocks = panel.reshape(window_len, cam_rows, FRONT * cam_rows)

    def inside_rest(position):
        return (position < window_len) & ((position < BAND - 1) | (position >= BAND - 1 + FRONT))

    update_mask = inside_rest(pos_home) & inside_rest(pos_other)
    pick_home = (pos_home[:, None] == jnp.arange(window_len)[None, :]).astype(jnp.float32)
    pick_other = (pos_other[:, None] == jnp.arange(window_len)[None, :]).astype(jnp.float32)
    rows_home = jnp.einsum("sp,pra->sra", pick_home, panel_blocks, precision=PRECISE)
    rows_other = jnp.einsum("sp,pra->sra", pick_other, panel_blocks, precision=PRECISE)
    change = jnp.einsum("sra,sca->src", rows_home, rows_other, precision=PRECISE)
    tiles_out = owned - jnp.where(update_mask[:, None, None], change, 0.0)
    solved_front = jax.scipy.linalg.solve_triangular(
        factor, window_rhs[BAND - 1 : BAND - 1 + FRONT].reshape(FRONT * cam_rows), lower=True
    )
    my_row = lax.dynamic_index_in_dim(
        panel_blocks, jnp.clip(my_pos, 0, window_len - 1), 0, keepdims=False
    )
    correction = reduced[0] - jnp.dot(my_row, solved_front, precision=PRECISE)
    front_piece = lax.dynamic_index_in_dim(
        solved_front.reshape(FRONT, cam_rows),
        jnp.clip(my_pos - (BAND - 1), 0, FRONT - 1),
        0,
        keepdims=False,
    )
    in_front = (my_pos >= BAND - 1) & (my_pos < BAND - 1 + FRONT)
    in_window = my_pos < window_len
    rhs_out = jnp.where(in_front, front_piece, jnp.where(in_window, correction, reduced[0]))[
        None, :
    ]
    return (tiles_out, rhs_out, front_panel)


def solution(mesh):
    in_specs = (
        P(("pts", "grp"), None, None, None, None),
        P(("pts", "grp"), None, None),
        P(("pts", "grp"), None, None),
        P(("pts", "grp"), None),
        P(),
        P(("pts", "grp"), None),
        P(),
        P(),
    )
    out_specs = (P(("pts", "grp"), None, None), P(("pts", "grp"), None), P(None, "grp"))
    return jax.shard_map(
        per_device, mesh=mesh, in_specs=in_specs, out_specs=out_specs, check_vma=False
    )
```

profile of v0, /device:TPU:0, one launch (start us, length us, event | category | flops | bytes accessed | tf_op | source)
XLA Modules:
  0.0 489.5 jit_solution(7508762552952673536)
XLA Ops:
  8.0 1.7 copy.43
  10.6 1.1 pad_maximum_fusion.1
  11.7 2.1 copy.46
  13.9 2.0 copy.44
  18.5 3.5 convolution_bitcast_fusion
  22.0 2.9 gather_fusion
  24.9 2.2 copy.49
  27.1 4.4 all-to-all-start
  32.1 5.0 %fusion.120 = s32[60]{0:T(128)S(1)} fusion(s32[60]{0:T(128)S(1)} %copy-done.16, s32[60]{0:T(128)S(1)} %copy-done.15, s32[]{:T(128)} %bitcast.1, s32[]{:T(128)} %bitcast.2, s32[]{:T(128)} %bitcast.3, s32[]{:T(128)} %bitcast.4, s32[]{:T(128)} %bitcast.5, s32[]{:T(128)} %bitcast.6, s32[]{:T(128)} %bitcast.7, s32[]{:T(128)} %bitcast.8, s32[]{:T(128)S(6)} %mul.589), kind=kLoop, calls=%fused_computation.234 | loop fusion | flops 1860 | bytes 756 | tf_op jit(solution)/shard_map/add | solution.py:68
  37.1 25.7 %all-to-all-done = f32[36,128,128]{2,0,1:T(8,128)S(1)} async-done(((f32[36,128,128]{2,0,1:T(8,128)}), f32[36,128,128]{2,0,1:T(8,128)S(1)}, u32[]{:S(2)}, u32[]{:S(2)}) %all-to-all-start) | async-done | bytes 2359328 | tf_op jit(solution)/shard_map/all_to_all | solution.py:129
  63.3 2.7 fusion.12
  66.8 1.4 copy.52
  68.2 6.6 %all-to-all-start.1 = ((f32[88,32,128]{2,1,0:T(8,128)}), f32[88,32,128]{2,1,0:T(8,128)S(1)}, u32[]{:S(2)}, u32[]{:S(2)}) async-start(f32[88,32,128]{2,1,0:T(8,128)} %copy.52), calls=%async_computation.1 | async-start | bytes 2883584 | tf_op jit(solution)/shard_map/all_to_all | solution.py:146
  78.3 30.5 %all-to-all-done.1 = f32[88,32,128]{2,1,0:T(8,128)S(1)} async-done(((f32[88,32,128]{2,1,0:T(8,128)}), f32[88,32,128]{2,1,0:T(8,128)S(1)}, u32[]{:S(2)}, u32[]{:S(2)}) %all-to-all-start.1) | async-done | bytes 1441824 | tf_op jit(solution)/shard_map/all_to_all | solution.py:146
  108.8 1.5 fusion.21
  110.2 1.1 copy.54
  111.3 3.5 all-to-all-start.2
  114.8 10.1 %all-reduce.4.cloned.1.call-start = ((), (), s32[]{:S(2)}) async-start(), calls=%async_computation.3 | async-start | bytes 7864320 | tf_op jit(solution)/shard_map/psum | solution.py:192
  126.3 1.9 fusion.47
  128.2 2.0 bitcast_add_fusion
  130.2 3.1 copy.58
  134.7 3.5 fusion.148
  138.5 1.6 collective-permute-start.1
  140.1 2.2 collective-permute-start.2
  142.4 2.6 collective-permute-done
  145.8 1.8 collective-permute-start.6
  148.6 2.6 collective-permute-done.5
  151.3 38.8 %psum.15 = f32[18,128]{1,0:T(8,128)S(1)} all-reduce(f32[18,128]{1,0:T(8,128)S(1)} %broadcast_multiply_fusion), channel_id=1, replica_groups=mesh['pts'=8,'grp'=4] {'pts','grp'}, use_global_device_ids=true, to_apply=%region_10.11 | all-reduce | flops 2304 | bytes 18432 | tf_op jit(solution)/shard_map/psum | solution.py:192
  190.1 83.9 %all-reduce.4.cloned.1.call-done = f32[60,128,128]{2,1,0:T(8,128)} async-done(((f32[60,128,128]{2,1,0:T(8,128)}), f32[60,128,128]{2,1,0:T(8,128)}) %all-reduce.4.cloned.1.call-update) | async-done | bytes 3932176 | tf_op jit(solution)/shard_map/psum | solution.py:192
  274.0 4.5 concatenate.34
  278.5 5.2 %gather_fusion.1 = f32[72,128,128]{2,1,0:T(8,128)} fusion(f32[61,128,128]{2,1,0:T(8,128)} %concatenate.34, s32[1024]{0:T(1024)S(1)} %pad_clamp_fusion), kind=kCustom, calls=%fused_computation.1 | custom fusion | bytes 9437472 | tf_op jit(solution)/shard_map/gather | solution.py:206
  283.7 1.3 slice.265
  286.4 1.6 copy.60
  289.2 11.7 %cholesky.86 = f32[128,128]{1,0:T(8,128)S(1)} custom-call(f32[128,128]{1,0:T(8,128)S(1)} %cholesky.232), custom_call_target="Cholesky" | custom-call | tf_op jit(solution)/shard_map/jit(cholesky)/cholesky | solution.py:211
  301.1 6.5 %copy.75 = f32[18,128,4,128]{1,0,3,2:T(8,128)} copy(f32[18,128,4,128]{3,1,2,0:T(8,128)} %bitcast.269) | data formatting | bytes 9437184 | tf_op jit(solution)/shard_map/reshape | solution.py:208
  307.6 9.8 %custom-call.34 = f32[1,128,128]{1,2,0:T(8,128)S(1)} custom-call(f32[1,128,128]{2,1,0:T(8,128)S(1)} %get-tuple-element.50), custom_call_target="InvertDiagBlocksLowerTriangular" | custom-call | tf_op jit(solution)/shard_map/jit(cholesky)/cholesky | solution.py:211
  318.1 11.7 %cholesky.183 = f32[128,128]{1,0:T(8,128)S(1)} custom-call(f32[128,128]{1,0:T(8,128)S(1)} %cholesky.236), custom_call_target="Cholesky" | custom-call | tf_op jit(solution)/shard_map/jit(cholesky)/cholesky | solution.py:211
  331.2 9.8 %custom-call.35 = f32[1,128,128]{1,2,0:T(8,128)S(1)} custom-call(f32[1,128,128]{2,1,0:T(8,128)S(1)} %get-tuple-element.47), custom_call_target="InvertDiagBlocksLowerTriangular" | custom-call | tf_op jit(solution)/shard_map/jit(cholesky)/cholesky | solution.py:211
  341.6 12.1 %cholesky.204 = f32[128,128]{1,0:T(8,128)S(1)} custom-call(f32[128,128]{1,0:T(8,128)S(1)} %cholesky.241), custom_call_target="Cholesky" | custom-call | tf_op jit(solution)/shard_map/jit(cholesky)/cholesky | solution.py:211
  354.4 9.8 %custom-call.36 = f32[1,128,128]{1,2,0:T(8,128)S(1)} custom-call(f32[1,128,128]{2,1,0:T(8,128)S(1)} %get-tuple-element.44), custom_call_target="InvertDiagBlocksLowerTriangular" | custom-call | tf_op jit(solution)/shard_map/jit(cholesky)/cholesky | solution.py:211
  364.8 11.7 %cholesky.221 = f32[128,128]{1,0:T(8,128)S(1)} custom-call(f32[128,128]{1,0:T(8,128)S(1)} %convolution_subtract_fusion.5), custom_call_target="Cholesky" | custom-call | tf_op jit(solution)/shard_map/jit(cholesky)/cholesky | solution.py:211
  379.9 8.0 %while.1 = (s32[]{:T(128)}, f32[512,512]{1,0:T(8,128)S(1)}, s32[4,2]{0,1:T(2,128)S(1)}, f32[4,128,128]{2,1,0:T(8,128)S(1)}, s32[]{:T(128)}) while((s32[]{:T(128)}, f32[512,512]{1,0:T(8,128)S(1)}, s32[4,2]{0,1:T(2,128)S(1)}, f32[4,128,128]{2,1,0:T(8,128)S(1)}, s32[]{:T(128)}) %tuple.64), condition=%wide.while_cond, body=%wide.while_body.sunk | while | flops 2 | bytes 131181 | solution.py:212
  380.5 1.4 bitcast_dynamic-update-slice_fusion.2
  382.5 1.4 bitcast_dynamic-update-slice_fusion.2
  384.5 1.4 bitcast_dynamic-update-slice_fusion.2
  386.5 1.4 bitcast_dynamic-update-slice_fusion.2
  387.9 39.5 %custom-call.37 = f32[4,128,128]{1,2,0:T(8,128)S(1)} custom-call(f32[4,128,128]{2,1,0:T(8,128)S(1)} %get-tuple-element.10), custom_call_target="InvertDiagBlocksLowerTriangular" | custom-call | tf_op jit(solution)/shard_map/jit(_solve_triangular)/triangular_solve | solution.py:212
  427.4 3.8 copy.113
  431.2 1.1 fusion.33
  432.4 1.2 convolution_subtract_fusion.2
  433.6 1.1 fusion.68
  434.7 1.4 convolution_subtract_fusion
  436.1 1.1 fusion.69
  437.2 2.2 convolution_subtract_fusion.1
  439.5 1.2 fusion.70
  440.6 4.3 pad_maximum_fusion
  444.9 6.1 %copy.63 = f32[2304,512]{1,0:T(8,128)} copy(f32[2304,512]{0,1:T(8,128)} %get-tuple-element.37) | data formatting | bytes 9437184 | tf_op jit(solution)/shard_map/transpose | solution.py:212
  451.0 7.7 %fusion.2 = f32[8,128,512]{2,0,1:T(8,128)S(1)} fusion(f32[18,128,512]{2,1,0:T(8,128)} %bitcast.264, s32[8]{0:T(128)S(1)} %get-tuple-element.30), kind=kOutput, calls=%fused_computation.6 | convolution fusion | flops 113246352 | bytes 6815776 | tf_op jit(solution)/shard_map/sp,pra->sra/dot_general | solution.py:223
  458.6 5.9 %fusion = f32[8,128,512]{2,0,1:T(8,128)} fusion(f32[18,128,512]{2,1,0:T(8,128)S(1)} %bitcast.266, s32[8]{0:T(128)S(1)} %get-tuple-element.29), kind=kOutput, calls=%fused_computation.4 | convolution fusion | flops 113246352 | bytes 6815776 | tf_op jit(solution)/shard_map/sp,pra->sra/dot_general | solution.py:224
  467.3 1.2 fusion.44
  468.7 2.4 dynamic-slice_bitcast_fusion
  471.1 2.7 copy.68
  473.8 6.7 %fusion.28 = f32[8,128,128]{2,1,0:T(8,128)} fusion(f32[8,128,128]{2,1,0:T(8,128)S(1)} %bitcast_add_fusion.2, f32[8,128,512]{2,0,1:T(8,128)} %fusion, f32[8,128,512]{2,0,1:T(8,128)S(1)} %fusion.2, pred[8]{0:T(512)(128)(4,1)S(1)} %get-tuple-element.28), kind=kOutput, calls=%fused_computation.37 | convolution fusion | flops 805568512 | bytes 5242888 | tf_op jit(solution)/shard_map/sra,sca->src/dot_general | solution.py:225
  480.5 1.8 fusion.42
  (118 shorter events, 26.9 us)
Async XLA Ops:
  7.2 118.4 %copy-start = (f32[32,128]{1,0:T(8,128)S(1)}, f32[32,128]{1,0:T(8,128)}, u32[]{:S(2)}) copy-start(f32[32,128]{1,0:T(8,128)} %param.21) | copy-start | bytes 49156
  13.8 2.0 copy-start.17
  15.8 1.4 copy-start.5
  17.2 1.2 copy-start.3
  18.5 3.5 copy-start.9
  27.1 4.4 copy-start.11
  27.1 5.0 %copy-start.15 = (s32[60]{0:T(128)S(1)}, s32[60]{0:T(128)}, u32[]{:S(2)}) copy-start(s32[60]{0:T(128)} %constant.368.clone) | copy-start | bytes 724
  27.1 5.0 %copy-start.16 = (s32[60]{0:T(128)S(1)}, s32[60]{0:T(128)}, u32[]{:S(2)}) copy-start(s32[60]{0:T(128)} %constant.369.clone) | copy-start | bytes 724
  27.1 35.7 %all-to-all-start = ((f32[36,128,128]{2,0,1:T(8,128)}), f32[36,128,128]{2,0,1:T(8,128)S(1)}, u32[]{:S(2)}, u32[]{:S(2)}) async-start(f32[36,128,128]{2,0,1:T(8,128)} %copy.49), calls=%async_computation | async-start | bytes 5242880 | tf_op jit(solution)/shard_map/all_to_all | solution.py:129
  37.1 26.2 %copy-start.10 = (f32[60,144,1]{1,0,2:T(8,128)S(1)}, f32[60,144,1]{1,0,2:T(8,128)}, u32[]{:S(2)}) copy-start(f32[60,144,1]{1,0,2:T(8,128)} %constant.431) | copy-start | bytes 103684
  68.2 40.5 %all-to-all-start.1 = ((f32[88,32,128]{2,1,0:T(8,128)}), f32[88,32,128]{2,1,0:T(8,128)S(1)}, u32[]{:S(2)}, u32[]{:S(2)}) async-start(f32[88,32,128]{2,1,0:T(8,128)} %copy.52), calls=%async_computation.1 | async-start | bytes 2883584 | tf_op jit(solution)/shard_map/all_to_all | solution.py:146
  111.3 14.4 %all-to-all-start.2 = ((f32[32,32,128]{2,1,0:T(8,128)}), f32[32,32,128]{2,1,0:T(8,128)S(1)}, u32[]{:S(2)}, u32[]{:S(2)}) async-start(f32[32,32,128]{2,1,0:T(8,128)} %copy.54), calls=%async_computation.2 | async-start | bytes 1048576 | tf_op jit(solution)/shard_map/all_to_all | solution.py:157
  114.8 159.2 %all-reduce.4.cloned.1.call-start = ((), (), s32[]{:S(2)}) async-start(), calls=%async_computation.3 | async-start | bytes 7864320 | tf_op jit(solution)/shard_map/psum | solution.py:192
  133.3 0.7 copy-start.12
  133.3 1.4 copy-start.4
  133.9 8.4 %copy-start.14 = (s32[72]{0:T(128)S(1)}, s32[72]{0:T(128)}, u32[]{:S(2)}) copy-start(s32[72]{0:T(128)} %constant.430) | copy-start | bytes 868
  133.9 17.3 %copy-start.13 = (f32[1,128]{1,0:T(1,128)S(1)}, f32[1,128]{1,0:T(1,128)}, u32[]{:S(2)}) copy-start(f32[1,128]{1,0:T(1,128)} %param.20) | copy-start | bytes 1540
  138.3 6.6 %collective-permute-start = (f32[128]{0:T(128)S(1)}, f32[128]{0:T(128)S(1)}, u32[]{:S(2)}, u32[]{:S(2)}) collective-permute-start(f32[128]{0:T(128)S(1)} %get-tuple-element.57), channel_id=1, source_target_pairs={{0,1},{1,2},{2,3},{3,4},{4,5},{5,6},{6,7},{7,8},{8,9},{9,10},{10,1... | collective-permute-start | bytes 1544 | tf_op jit(solution)/shard_map/ppermute | solution.py:16
  138.5 7.3 %collective-permute-start.1 = (f32[128]{0:T(128)S(1)}, f32[128]{0:T(128)S(1)}, u32[]{:S(2)}, u32[]{:S(2)}) collective-permute-start(f32[128]{0:T(128)S(1)} %get-tuple-element.63), channel_id=1, source_target_pairs={{0,2},{1,3},{2,4},{3,5},{4,6},{5,7},{6,8},{7,9},{8,10},{9,11},{10,... | collective-permute-start | bytes 1544 | tf_op jit(solution)/shard_map/ppermute | solution.py:16
  140.1 7.4 %collective-permute-start.2 = (f32[128]{0:T(128)S(1)}, f32[128]{0:T(128)S(1)}, u32[]{:S(2)}, u32[]{:S(2)}) collective-permute-start(f32[128]{0:T(128)S(1)} %get-tuple-element.62), channel_id=1, source_target_pairs={{0,3},{1,4},{2,5},{3,6},{4,7},{5,8},{6,9},{7,10},{8,11},{9,12},{10... | collective-permute-start | bytes 1544 | tf_op jit(solution)/shard_map/ppermute | solution.py:16
  142.3 6.3 %collective-permute-start.3 = (f32[128]{0:T(128)S(1)}, f32[128]{0:T(128)S(1)}, u32[]{:S(2)}, u32[]{:S(2)}) collective-permute-start(f32[128]{0:T(128)S(1)} %get-tuple-element.61), channel_id=1, source_target_pairs={{0,4},{1,5},{2,6},{3,7},{4,8},{5,9},{6,10},{7,11},{8,12},{9,13},{1... | collective-permute-start | bytes 1544 | tf_op jit(solution)/shard_map/ppermute | solution.py:16
  142.3 6.3 %collective-permute-start.4 = (f32[128]{0:T(128)S(1)}, f32[128]{0:T(128)S(1)}, u32[]{:S(2)}, u32[]{:S(2)}) collective-permute-start(f32[128]{0:T(128)S(1)} %get-tuple-element.60), channel_id=1, source_target_pairs={{0,5},{1,6},{2,7},{3,8},{4,9},{5,10},{6,11},{7,12},{8,13},{9,14},{... | collective-permute-start | bytes 1544 | tf_op jit(solution)/shard_map/ppermute | solution.py:16
  144.9 6.3 %collective-permute-start.5 = (f32[128]{0:T(128)S(1)}, f32[128]{0:T(128)S(1)}, u32[]{:S(2)}, u32[]{:S(2)}) collective-permute-start(f32[128]{0:T(128)S(1)} %get-tuple-element.59), channel_id=1, source_target_pairs={{0,6},{1,7},{2,8},{3,9},{4,10},{5,11},{6,12},{7,13},{8,14},{9,15},... | collective-permute-start | bytes 1544 | tf_op jit(solution)/shard_map/ppermute | solution.py:16
  145.8 5.4 %collective-permute-start.6 = (f32[128]{0:T(128)S(1)}, f32[128]{0:T(128)S(1)}, u32[]{:S(2)}, u32[]{:S(2)}) collective-permute-start(f32[128]{0:T(128)S(1)} %get-tuple-element.58), channel_id=1, source_target_pairs={{0,7},{1,8},{2,9},{3,10},{4,11},{5,12},{6,13},{7,14},{8,15},{9,16}... | collective-permute-start | bytes 1544 | tf_op jit(solution)/shard_map/ppermute | solution.py:16
  288.2 1.0 copy-start.7
  301.1 16.4 %copy-start.8 = (f32[512,512]{1,0:T(8,128)S(1)}, f32[512,512]{1,0:T(8,128)}, u32[]{:S(2)}) copy-start(f32[512,512]{1,0:T(8,128)} %copy-done.7) | copy-start | bytes 3145732
  387.9 49.3 %copy-start.6 = (f32[512,512]{1,0:T(8,128)}, f32[512,512]{1,0:T(8,128)S(1)}, u32[]{:S(2)}) copy-start(f32[512,512]{1,0:T(8,128)S(1)} %get-tuple-element.133) | copy-start | bytes 3145732
  451.0 7.7 %copy-start.2 = (f32[2304,512]{1,0:T(8,128)S(1)}, f32[2304,512]{1,0:T(8,128)}, u32[]{:S(2)}) copy-start(f32[2304,512]{1,0:T(8,128)} %copy.63) | copy-start | bytes 14155780
  473.8 8.5 %copy-start.1 = (f32[32,128]{1,0:T(8,128)S(1)}, f32[32,128]{1,0:T(8,128)}, u32[]{:S(2)}) copy-start(f32[32,128]{1,0:T(8,128)} %param.21) | copy-start | bytes 49156
Sparse Core Ops, SparseCore 0:
  133.4 140.5 all-reduce.3
where the time goes:
time: 499 us; the launch traced here: 490 us
  waiting for transfers between devices  147 us (29%)
  other arithmetic  134 us (27%)
  local copies, waits for them, and re-layouts  66.2 us (13%)
  matrix products  54.6 us (11%)
  blocking collectives  38.8 us (8%)
  starting transfers between devices  30.4 us (6%)
  between operations  18.1 us (4%)
    psum x1, waiting for transfers between devices, per_device(): front_rows, window_rhs = lax.psum((front_rows, window_rhs), ('pts', 'grp'))  83.9 us
    another operation x15, other arithmetic, per_device(): factor = jnp.linalg.cholesky(square)  79.4 us
    another operation x4, other arithmetic, per_device(): panel = jax.scipy.linalg.solve_triangular(factor, columns.T, lower=True).T  43.9 us
    psum x1, blocking collectives, per_device(): front_rows, window_rhs = lax.psum((front_rows, window_rhs), ('pts', 'grp'))  38.8 us
    all_to_all x1, waiting for transfers between devices, per_device(): lax.all_to_all(outgoing, 'pts', split_axis=0, concat_axis=0, tiled=True)  30.5 us
    all_to_all x1, waiting for transfers between devices, per_device(): lax.all_to_all(band_tiles, 'grp', split_axis=1, concat_axis=0, tiled=True)  25.7 us
    unnamed x40, local copies, waits for them, and re-layouts  13.1 us
    psum x1, starting transfers between devices, per_device(): front_rows, window_rhs = lax.psum((front_rows, window_rhs), ('pts', 'grp'))  10.1 us
  transfers between devices with their start and end apart: 11, of which 7 were waited for; matrix products, arithmetic and copies ran while one was open for 3% of the time, Pallas kernels for 0%

commit v1 on v0

--- a/solution.py
+++ b/solution.py
@@ -8,6 +8,17 @@
 BAND = 8
 FRONT = 4
 PRECISE = lax.Precision.HIGHEST
+
+
+def in_blocks(x, dim, length):
+    before, after = (x.shape[:dim], x.shape[dim + 1 :])
+    return jnp.moveaxis(x.reshape(*before, length, -1, *after), dim, 0)
+
+
+def in_order(parts, dim):
+    shape = list(parts.shape[1:])
+    shape[dim] *= parts.shape[0]
+    return jnp.moveaxis(parts, 0, dim).reshape(shape)
 
 
 def shifted(value, axis, steps):
@@ -143,7 +154,15 @@
     outgoing, capacity = route_rows(
         union_rows, tile_owner, BAND * grp_count * my_pts, union_rows_list, union_offsets, pts_count
     )
-    incoming = lax.all_to_all(outgoing, "pts", split_axis=0, concat_axis=0, tiled=True)
+    size, place = (lax.axis_size("pts"), lax.axis_index("pts"))
+    pieces = in_blocks(outgoing, 0, size)
+    out = pieces
+    for turn in range(1, size):
+        target_2, source_2 = ((place + turn) % size, (place - turn) % size)
+        sent = lax.dynamic_index_in_dim(pieces, target_2, 0)
+        partner_block = lax.ppermute(sent, "pts", [(i, (i + turn) % size) for i in range(size)])
+        out = lax.dynamic_update_slice_in_dim(out, partner_block, source_2, axis=0)
+    incoming = in_order(out, 0)
     owner_rows = collect_rows(
         incoming,
         capacity,

time: 499 us -> 500 us (level)
  starting transfers between devices: 30.4 us -> 47.3 us
  waiting for transfers between devices: 147 us -> 134 us
    all_to_all x1 -> x0, waiting for transfers between devices: 30.5 us -> none  [per_device(): lax.all_to_all(outgoing, 'pts', split_axis=0, concat_axis=0, tiled=True)]
    ppermute x0 -> x7, starting transfers between devices: none -> 21.6 us  [per_device(): lax.ppermute(sent, 'pts', [(i, (i + turn) % size) for i in range(size)])]
    ppermute x0 -> x7, waiting for transfers between devices: none -> 12.5 us  [per_device(): lax.ppermute(sent, 'pts', [(i, (i + turn) % size) for i in range(size)])]
    ppermute x7, starting transfers between devices: 5.81 us -> 17.8 us  [shifted(): return lax.ppermute(value, axis, pairs)]
    psum x1, starting transfers between devices: 10.1 us -> 0.04 us  [per_device(): front_rows, window_rhs = lax.psum((front_rows, window_rhs), ('pts', 'grp'))]
    all_to_all x1, waiting for transfers between devices: 0.01 us -> 7.88 us  [per_device(): lax.all_to_all(owner_rows, 'grp', split_axis=0, concat_axis=1, tiled=True)]
    all_to_all x1 -> x0, starting transfers between devices: 6.65 us -> none  [per_device(): lax.all_to_all(outgoing, 'pts', split_axis=0, concat_axis=0, tiled=True)]
  transfers between devices with their start and end apart: 11 -> 17, of which waited for: 7 -> 9; matrix products, arithmetic and copies ran while one was open for 3% -> 3% of each run, Pallas kernels for 0% -> 0%
where the time goes in v1:
time: 500 us; the launch traced here: 492 us
  other arithmetic  134 us (27%)
  waiting for transfers between devices  134 us (27%)
  local copies, waits for them, and re-layouts  65.5 us (13%)
  matrix products  54.6 us (11%)
  starting transfers between devices  47.3 us (9%)
  blocking collectives  37 us (7%)
  between operations  18.5 us (4%)
    psum x1, waiting for transfers between devices, per_device(): front_rows, window_rhs = lax.psum((front_rows, window_rhs), ('pts', 'grp'))  85.1 us
    another operation x15, other arithmetic, per_device(): factor = jnp.linalg.cholesky(square)  79.2 us
    another operation x4, other arithmetic, per_device(): panel = jax.scipy.linalg.solve_triangular(factor, columns.T, lower=True).T  43.9 us
    psum x1, blocking collectives, per_device(): front_rows, window_rhs = lax.psum((front_rows, window_rhs), ('pts', 'grp'))  37 us
    all_to_all x1, waiting for transfers between devices, per_device(): lax.all_to_all(band_tiles, 'grp', split_axis=1, concat_axis=0, tiled=True)  23.5 us
    ppermute x7, starting transfers between devices, per_device(): lax.ppermute(sent, 'pts', [(i, (i + turn) % size) for i in range(size)])  21.6 us
    ppermute x7, starting transfers between devices, shifted(): return lax.ppermute(value, axis, pairs)  17.8 us
    unnamed x40, local copies, waits for them, and re-layouts  13.1 us
  transfers between devices with their start and end apart: 17, of which 9 were waited for; matrix products, arithmetic and copies ran while one was open for 3% of the time, Pallas kernels for 0%

profile of v1, /device:TPU:0, one launch (start us, length us, event | category | flops | bytes accessed | tf_op | source)
XLA Modules:
  0.0 491.6 jit_solution(8358686760833284133)
XLA Ops:
  8.0 1.7 copy.45
  11.7 2.1 copy.48
  13.9 2.0 copy.46
  18.5 3.5 convolution_bitcast_fusion
  22.0 2.9 gather_fusion
  24.9 2.2 copy.51
  27.1 4.4 all-to-all-start
  34.3 5.1 %fusion.120 = s32[60]{0:T(128)S(1)} fusion(s32[60]{0:T(128)S(1)} %copy-done.16, s32[60]{0:T(128)S(1)} %copy-done.15, s32[]{:T(128)} %bitcast.1, s32[]{:T(128)} %bitcast.2, s32[]{:T(128)} %bitcast.3, s32[]{:T(128)} %bitcast.4, s32[]{:T(128)} %bitcast.5, s32[]{:T(128)} %bitcast.6, s32[]{:T(128)} %bitcast.7, s32[]{:T(128)} %bitcast.8, s32[]{:T(128)S(6)} %mul.589), kind=kLoop, calls=%fused_computation.248 | loop fusion | flops 1860 | bytes 756 | tf_op jit(solution)/shard_map/add | solution.py:79
  39.3 23.5 %all-to-all-done = f32[36,128,128]{2,0,1:T(8,128)S(1)} async-done(((f32[36,128,128]{2,0,1:T(8,128)}), f32[36,128,128]{2,0,1:T(8,128)S(1)}, u32[]{:S(2)}, u32[]{:S(2)}) %all-to-all-start) | async-done | bytes 2359328 | tf_op jit(solution)/shard_map/all_to_all | solution.py:140
  63.3 2.7 fusion.12
  67.2 2.4 collective-permute-start
  69.6 7.2 %collective-permute-done = f32[1,11,32,128]{3,2,1,0:T(8,128)S(1)} collective-permute-done((f32[1,11,32,128]{3,2,1,0:T(8,128)S(1)}, f32[1,11,32,128]{3,2,1,0:T(8,128)S(1)}, u32[]{:S(2)}, u32[]{:S(2)}) %collective-permute-start) | collective-permute-done | bytes 180256 | tf_op jit(solution)/shard_map/ppermute | solution.py:163
  77.7 1.3 collective-permute-start.2
  79.7 1.3 collective-permute-start.3
  81.0 3.5 collective-permute-start.4
  84.5 1.6 collective-permute-start.5
  86.4 11.4 %collective-permute-start.6 = (f32[1,11,32,128]{3,2,1,0:T(8,128)S(1)}, f32[1,11,32,128]{3,2,1,0:T(8,128)S(1)}, u32[]{:S(2)}, u32[]{:S(2)}) collective-permute-start(f32[1,11,32,128]{3,2,1,0:T(8,128)S(1)} %get-tuple-element.41), channel_id=1, source_target_pairs={{0,28},{4,0},{8,4},{12,8},{16,12},{20,16},{24,20},{28,24},{1,29},{... | collective-permute-start | bytes 540680 | tf_op jit(solution)/shard_map/ppermute | solution.py:163
  97.8 2.1 collective-permute-done.3
  100.0 2.9 collective-permute-done.6
  102.9 1.5 fusion.21
  105.5 3.5 all-to-all-start.1
  109.8 7.9 %all-to-all-done.1 = f32[32,32,128]{2,1,0:T(8,128)S(1)} async-done(((f32[32,32,128]{2,1,0:T(8,128)}), f32[32,32,128]{2,1,0:T(8,128)S(1)}, u32[]{:S(2)}, u32[]{:S(2)}) %all-to-all-start.1) | async-done | bytes 524320 | tf_op jit(solution)/shard_map/all_to_all | solution.py:176
  118.2 1.9 fusion.47
  120.1 2.0 bitcast_add_fusion
  122.2 3.1 copy.60
  126.7 3.5 fusion.148
  130.3 5.9 %collective-permute-start.10 = (f32[128]{0:T(128)S(1)}, f32[128]{0:T(128)S(1)}, u32[]{:S(2)}, u32[]{:S(2)}) collective-permute-start(f32[128]{0:T(128)S(1)} %get-tuple-element.68), channel_id=1, source_target_pairs={{0,4},{1,5},{2,6},{3,7},{4,8},{5,9},{6,10},{7,11},{8,12},{9,13},{1... | collective-permute-start | bytes 1544 | tf_op jit(solution)/shard_map/ppermute | solution.py:27
  136.1 5.1 %collective-permute-start.12 = (f32[128]{0:T(128)S(1)}, f32[128]{0:T(128)S(1)}, u32[]{:S(2)}, u32[]{:S(2)}) collective-permute-start(f32[128]{0:T(128)S(1)} %get-tuple-element.66), channel_id=1, source_target_pairs={{0,6},{1,7},{2,8},{3,9},{4,10},{5,11},{6,12},{7,13},{8,14},{9,15},... | collective-permute-start | bytes 1544 | tf_op jit(solution)/shard_map/ppermute | solution.py:27
  141.3 5.0 %collective-permute-start.13 = (f32[128]{0:T(128)S(1)}, f32[128]{0:T(128)S(1)}, u32[]{:S(2)}, u32[]{:S(2)}) collective-permute-start(f32[128]{0:T(128)S(1)} %get-tuple-element.65), channel_id=1, source_target_pairs={{0,7},{1,8},{2,9},{3,10},{4,11},{5,12},{6,13},{7,14},{8,15},{9,16}... | collective-permute-start | bytes 1544 | tf_op jit(solution)/shard_map/ppermute | solution.py:27
  146.7 1.5 collective-permute-start.9
  148.2 4.7 collective-permute-done.7
  153.7 37.0 %psum.15 = f32[18,128]{1,0:T(8,128)S(1)} all-reduce(f32[18,128]{1,0:T(8,128)S(1)} %broadcast_multiply_fusion), channel_id=1, replica_groups=mesh['pts'=8,'grp'=4] {'pts','grp'}, use_global_device_ids=true, to_apply=%region_10.11 | all-reduce | flops 2304 | bytes 18432 | tf_op jit(solution)/shard_map/psum | solution.py:211
  190.7 85.1 %all-reduce.4.cloned.1.call-done = f32[60,128,128]{2,1,0:T(8,128)} async-done(((f32[60,128,128]{2,1,0:T(8,128)}), f32[60,128,128]{2,1,0:T(8,128)}) %all-reduce.4.cloned.1.call-update) | async-done | bytes 3932176 | tf_op jit(solution)/shard_map/psum | solution.py:211
  275.8 4.5 concatenate.34
  280.4 5.2 %gather_fusion.1 = f32[72,128,128]{2,1,0:T(8,128)} fusion(f32[61,128,128]{2,1,0:T(8,128)} %concatenate.34, s32[1024]{0:T(1024)S(1)} %pad_clamp_fusion), kind=kCustom, calls=%fused_computation.1 | custom fusion | bytes 9437472 | tf_op jit(solution)/shard_map/gather | solution.py:225
  285.6 1.3 slice.265
  288.3 1.6 copy.62
  291.1 11.7 %cholesky.86 = f32[128,128]{1,0:T(8,128)S(1)} custom-call(f32[128,128]{1,0:T(8,128)S(1)} %cholesky.232), custom_call_target="Cholesky" | custom-call | tf_op jit(solution)/shard_map/jit(cholesky)/cholesky | solution.py:230
  303.0 6.7 %copy.77 = f32[18,128,4,128]{1,0,3,2:T(8,128)} copy(f32[18,128,4,128]{3,1,2,0:T(8,128)} %bitcast.271) | data formatting | bytes 9437184 | tf_op jit(solution)/shard_map/reshape | solution.py:227
  309.7 9.8 %custom-call.34 = f32[1,128,128]{1,2,0:T(8,128)S(1)} custom-call(f32[1,128,128]{2,1,0:T(8,128)S(1)} %get-tuple-element.57), custom_call_target="InvertDiagBlocksLowerTriangular" | custom-call | tf_op jit(solution)/shard_map/jit(cholesky)/cholesky | solution.py:230
  320.2 11.7 %cholesky.183 = f32[128,128]{1,0:T(8,128)S(1)} custom-call(f32[128,128]{1,0:T(8,128)S(1)} %cholesky.236), custom_call_target="Cholesky" | custom-call | tf_op jit(solution)/shard_map/jit(cholesky)/cholesky | solution.py:230
  333.2 9.8 %custom-call.35 = f32[1,128,128]{1,2,0:T(8,128)S(1)} custom-call(f32[1,128,128]{2,1,0:T(8,128)S(1)} %get-tuple-element.54), custom_call_target="InvertDiagBlocksLowerTriangular" | custom-call | tf_op jit(solution)/shard_map/jit(cholesky)/cholesky | solution.py:230
  343.7 11.9 %cholesky.204 = f32[128,128]{1,0:T(8,128)S(1)} custom-call(f32[128,128]{1,0:T(8,128)S(1)} %cholesky.241), custom_call_target="Cholesky" | custom-call | tf_op jit(solution)/shard_map/jit(cholesky)/cholesky | solution.py:230
  356.2 9.8 %custom-call.36 = f32[1,128,128]{1,2,0:T(8,128)S(1)} custom-call(f32[1,128,128]{2,1,0:T(8,128)S(1)} %get-tuple-element.51), custom_call_target="InvertDiagBlocksLowerTriangular" | custom-call | tf_op jit(solution)/shard_map/jit(cholesky)/cholesky | solution.py:230
  366.7 11.7 %cholesky.221 = f32[128,128]{1,0:T(8,128)S(1)} custom-call(f32[128,128]{1,0:T(8,128)S(1)} %convolution_subtract_fusion.5), custom_call_target="Cholesky" | custom-call | tf_op jit(solution)/shard_map/jit(cholesky)/cholesky | solution.py:230
  381.9 8.0 %while.1 = (s32[]{:T(128)}, f32[512,512]{1,0:T(8,128)S(1)}, s32[4,2]{0,1:T(2,128)S(1)}, f32[4,128,128]{2,1,0:T(8,128)S(1)}, s32[]{:T(128)}) while((s32[]{:T(128)}, f32[512,512]{1,0:T(8,128)S(1)}, s32[4,2]{0,1:T(2,128)S(1)}, f32[4,128,128]{2,1,0:T(8,128)S(1)}, s32[]{:T(128)}) %tuple.70), condition=%wide.while_cond, body=%wide.while_body.sunk | while | flops 2 | bytes 131181 | solution.py:231
  382.5 1.4 bitcast_dynamic-update-slice_fusion.2
  384.5 1.4 bitcast_dynamic-update-slice_fusion.2
  386.5 1.4 bitcast_dynamic-update-slice_fusion.2
  388.5 1.4 bitcast_dynamic-update-slice_fusion.2
  389.9 39.5 %custom-call.37 = f32[4,128,128]{1,2,0:T(8,128)S(1)} custom-call(f32[4,128,128]{2,1,0:T(8,128)S(1)} %get-tuple-element.10), custom_call_target="InvertDiagBlocksLowerTriangular" | custom-call | tf_op jit(solution)/shard_map/jit(_solve_triangular)/triangular_solve | solution.py:231
  429.5 3.8 copy.115
  434.4 1.2 convolution_subtract_fusion.2
  436.8 1.4 convolution_subtract_fusion
  439.3 2.2 convolution_subtract_fusion.1
  442.7 4.2 pad_maximum_fusion
  446.9 6.1 %copy.65 = f32[2304,512]{1,0:T(8,128)} copy(f32[2304,512]{0,1:T(8,128)} %get-tuple-element.37) | data formatting | bytes 9437184 | tf_op jit(solution)/shard_map/transpose | solution.py:231
  453.0 7.7 %fusion.2 = f32[8,128,512]{2,0,1:T(8,128)S(1)} fusion(f32[18,128,512]{2,1,0:T(8,128)} %bitcast.266, s32[8]{0:T(128)S(1)} %get-tuple-element.30), kind=kOutput, calls=%fused_computation.6 | convolution fusion | flops 113246352 | bytes 6815776 | tf_op jit(solution)/shard_map/sp,pra->sra/dot_general | solution.py:242
  460.7 5.9 %fusion = f32[8,128,512]{2,0,1:T(8,128)} fusion(f32[18,128,512]{2,1,0:T(8,128)S(1)} %bitcast.268, s32[8]{0:T(128)S(1)} %get-tuple-element.29), kind=kOutput, calls=%fused_computation.4 | convolution fusion | flops 113246352 | bytes 6815776 | tf_op jit(solution)/shard_map/sp,pra->sra/dot_general | solution.py:243
  469.3 1.2 fusion.44
  470.8 2.4 dynamic-slice_bitcast_fusion
  473.2 2.7 copy.70
  475.8 6.7 %fusion.28 = f32[8,128,128]{2,1,0:T(8,128)} fusion(f32[8,128,128]{2,1,0:T(8,128)S(1)} %bitcast_add_fusion.2, f32[8,128,512]{2,0,1:T(8,128)} %fusion, f32[8,128,512]{2,0,1:T(8,128)S(1)} %fusion.2, pred[8]{0:T(512)(128)(4,1)S(1)} %get-tuple-element.28), kind=kOutput, calls=%fused_computation.37 | convolution fusion | flops 805568512 | bytes 5242888 | tf_op jit(solution)/shard_map/sra,sca->src/dot_general | solution.py:244
  482.5 1.8 fusion.42
  (138 shorter events, 33.5 us)
Async XLA Ops:
  7.2 102.5 %copy-start = (f32[32,128]{1,0:T(8,128)S(1)}, f32[32,128]{1,0:T(8,128)}, u32[]{:S(2)}) copy-start(f32[32,128]{1,0:T(8,128)} %param.21) | copy-start | bytes 49156
  13.8 2.0 copy-start.17
  15.8 1.4 copy-start.5
  17.2 1.3 copy-start.3
  18.5 3.5 copy-start.9
  27.1 5.1 %copy-start.11 = (s32[8]{0:T(128)S(1)}, s32[8]{0:T(128)}, u32[]{:S(2)}) copy-start(s32[8]{0:T(128)} %param.23) | copy-start | bytes 100
  27.1 7.1 %copy-start.15 = (s32[60]{0:T(128)S(1)}, s32[60]{0:T(128)}, u32[]{:S(2)}) copy-start(s32[60]{0:T(128)} %constant.459.clone) | copy-start | bytes 724
  27.1 7.1 %copy-start.16 = (s32[60]{0:T(128)S(1)}, s32[60]{0:T(128)}, u32[]{:S(2)}) copy-start(s32[60]{0:T(128)} %constant.460.clone) | copy-start | bytes 724
  27.1 35.7 %all-to-all-start = ((f32[36,128,128]{2,0,1:T(8,128)}), f32[36,128,128]{2,0,1:T(8,128)S(1)}, u32[]{:S(2)}, u32[]{:S(2)}) async-start(f32[36,128,128]{2,0,1:T(8,128)} %copy.51), calls=%async_computation | async-start | bytes 5242880 | tf_op jit(solution)/shard_map/all_to_all | solution.py:140
  39.3 24.0 %copy-start.10 = (f32[60,144,1]{1,0,2:T(8,128)S(1)}, f32[60,144,1]{1,0,2:T(8,128)}, u32[]{:S(2)}) copy-start(f32[60,144,1]{1,0,2:T(8,128)} %constant.522) | copy-start | bytes 103684
  67.2 9.7 %collective-permute-start = (f32[1,11,32,128]{3,2,1,0:T(8,128)S(1)}, f32[1,11,32,128]{3,2,1,0:T(8,128)S(1)}, u32[]{:S(2)}, u32[]{:S(2)}) collective-permute-start(f32[1,11,32,128]{3,2,1,0:T(8,128)S(1)} %constant_dynamic-slice_fusion.8), channel_id=1, source_target_pairs={{0,4},{4,8},{8,12},{12,16},{16,20},{20,24},{24,28},{28,0},{1,5},{5... | collective-permute-start | bytes 540680 | tf_op jit(solution)/shard_map/ppermute | solution.py:163
  77.0 9.4 %collective-permute-start.1 = (f32[1,11,32,128]{3,2,1,0:T(8,128)S(1)}, f32[1,11,32,128]{3,2,1,0:T(8,128)S(1)}, u32[]{:S(2)}, u32[]{:S(2)}) collective-permute-start(f32[1,11,32,128]{3,2,1,0:T(8,128)S(1)} %get-tuple-element.46), channel_id=1, source_target_pairs={{0,8},{4,12},{8,16},{12,20},{16,24},{20,28},{24,0},{28,4},{1,9},{5... | collective-permute-start | bytes 540680 | tf_op jit(solution)/shard_map/ppermute | solution.py:163
  77.7 20.1 %collective-permute-start.2 = (f32[1,11,32,128]{3,2,1,0:T(8,128)S(1)}, f32[1,11,32,128]{3,2,1,0:T(8,128)S(1)}, u32[]{:S(2)}, u32[]{:S(2)}) collective-permute-start(f32[1,11,32,128]{3,2,1,0:T(8,128)S(1)} %get-tuple-element.45), channel_id=1, source_target_pairs={{0,12},{4,16},{8,20},{12,24},{16,28},{20,0},{24,4},{28,8},{1,13},{... | collective-permute-start | bytes 540680 | tf_op jit(solution)/shard_map/ppermute | solution.py:163
  79.7 20.2 %collective-permute-start.3 = (f32[1,11,32,128]{3,2,1,0:T(8,128)S(1)}, f32[1,11,32,128]{3,2,1,0:T(8,128)S(1)}, u32[]{:S(2)}, u32[]{:S(2)}) collective-permute-start(f32[1,11,32,128]{3,2,1,0:T(8,128)S(1)} %get-tuple-element.44), channel_id=1, source_target_pairs={{0,16},{4,20},{8,24},{12,28},{16,0},{20,4},{24,8},{28,12},{1,17},{... | collective-permute-start | bytes 540680 | tf_op jit(solution)/shard_map/ppermute | solution.py:163
  81.0 18.9 %collective-permute-start.4 = (f32[1,11,32,128]{3,2,1,0:T(8,128)S(1)}, f32[1,11,32,128]{3,2,1,0:T(8,128)S(1)}, u32[]{:S(2)}, u32[]{:S(2)}) collective-permute-start(f32[1,11,32,128]{3,2,1,0:T(8,128)S(1)} %get-tuple-element.43), channel_id=1, source_target_pairs={{0,20},{4,24},{8,28},{12,0},{16,4},{20,8},{24,12},{28,16},{1,21},{... | collective-permute-start | bytes 540680 | tf_op jit(solution)/shard_map/ppermute | solution.py:163
  84.5 15.4 %collective-permute-start.5 = (f32[1,11,32,128]{3,2,1,0:T(8,128)S(1)}, f32[1,11,32,128]{3,2,1,0:T(8,128)S(1)}, u32[]{:S(2)}, u32[]{:S(2)}) collective-permute-start(f32[1,11,32,128]{3,2,1,0:T(8,128)S(1)} %get-tuple-element.42), channel_id=1, source_target_pairs={{0,24},{4,28},{8,0},{12,4},{16,8},{20,12},{24,16},{28,20},{1,25},{... | collective-permute-start | bytes 540680 | tf_op jit(solution)/shard_map/ppermute | solution.py:163
  86.4 16.5 %collective-permute-start.6 = (f32[1,11,32,128]{3,2,1,0:T(8,128)S(1)}, f32[1,11,32,128]{3,2,1,0:T(8,128)S(1)}, u32[]{:S(2)}, u32[]{:S(2)}) collective-permute-start(f32[1,11,32,128]{3,2,1,0:T(8,128)S(1)} %get-tuple-element.41), channel_id=1, source_target_pairs={{0,28},{4,0},{8,4},{12,8},{16,12},{20,16},{24,20},{28,24},{1,29},{... | collective-permute-start | bytes 540680 | tf_op jit(solution)/shard_map/ppermute | solution.py:163
  105.5 12.3 %all-to-all-start.1 = ((f32[32,32,128]{2,1,0:T(8,128)}), f32[32,32,128]{2,1,0:T(8,128)S(1)}, u32[]{:S(2)}, u32[]{:S(2)}) async-start(f32[32,32,128]{2,1,0:T(8,128)} %copy.56), calls=%async_computation.1 | async-start | bytes 1048576 | tf_op jit(solution)/shard_map/all_to_all | solution.py:176
  108.9 166.9 %all-reduce.4.cloned.1.call-start = ((), (), s32[]{:S(2)}) async-start(), calls=%async_computation.2 | async-start | bytes 7864320 | tf_op jit(solution)/shard_map/psum | solution.py:211
  125.2 0.7 copy-start.12
  125.2 1.4 copy-start.4
  125.9 20.4 %copy-start.14 = (s32[72]{0:T(128)S(1)}, s32[72]{0:T(128)}, u32[]{:S(2)}) copy-start(s32[72]{0:T(128)} %constant.521) | copy-start | bytes 868
  125.9 27.7 %copy-start.13 = (f32[1,128]{1,0:T(1,128)S(1)}, f32[1,128]{1,0:T(1,128)}, u32[]{:S(2)}) copy-start(f32[1,128]{1,0:T(1,128)} %param.20) | copy-start | bytes 1540
  130.3 16.1 %collective-permute-start.10 = (f32[128]{0:T(128)S(1)}, f32[128]{0:T(128)S(1)}, u32[]{:S(2)}, u32[]{:S(2)}) collective-permute-start(f32[128]{0:T(128)S(1)} %get-tuple-element.68), channel_id=1, source_target_pairs={{0,4},{1,5},{2,6},{3,7},{4,8},{5,9},{6,10},{7,11},{8,12},{9,13},{1... | collective-permute-start | bytes 1544 | tf_op jit(solution)/shard_map/ppermute | solution.py:27
  136.1 10.5 %collective-permute-start.11 = (f32[128]{0:T(128)S(1)}, f32[128]{0:T(128)S(1)}, u32[]{:S(2)}, u32[]{:S(2)}) collective-permute-start(f32[128]{0:T(128)S(1)} %get-tuple-element.67), channel_id=1, source_target_pairs={{0,5},{1,6},{2,7},{3,8},{4,9},{5,10},{6,11},{7,12},{8,13},{9,14},{... | collective-permute-start | bytes 1544 | tf_op jit(solution)/shard_map/ppermute | solution.py:27
  136.1 12.0 %collective-permute-start.12 = (f32[128]{0:T(128)S(1)}, f32[128]{0:T(128)S(1)}, u32[]{:S(2)}, u32[]{:S(2)}) collective-permute-start(f32[128]{0:T(128)S(1)} %get-tuple-element.66), channel_id=1, source_target_pairs={{0,6},{1,7},{2,8},{3,9},{4,10},{5,11},{6,12},{7,13},{8,14},{9,15},... | collective-permute-start | bytes 1544 | tf_op jit(solution)/shard_map/ppermute | solution.py:27
  141.3 6.9 %collective-permute-start.13 = (f32[128]{0:T(128)S(1)}, f32[128]{0:T(128)S(1)}, u32[]{:S(2)}, u32[]{:S(2)}) collective-permute-start(f32[128]{0:T(128)S(1)} %get-tuple-element.65), channel_id=1, source_target_pairs={{0,7},{1,8},{2,9},{3,10},{4,11},{5,12},{6,13},{7,14},{8,15},{9,16}... | collective-permute-start | bytes 1544 | tf_op jit(solution)/shard_map/ppermute | solution.py:27
  146.3 6.6 %collective-permute-start.7 = (f32[128]{0:T(128)S(1)}, f32[128]{0:T(128)S(1)}, u32[]{:S(2)}, u32[]{:S(2)}) collective-permute-start(f32[128]{0:T(128)S(1)} %get-tuple-element.64), channel_id=1, source_target_pairs={{0,1},{1,2},{2,3},{3,4},{4,5},{5,6},{6,7},{7,8},{8,9},{9,10},{10,1... | collective-permute-start | bytes 1544 | tf_op jit(solution)/shard_map/ppermute | solution.py:27
  146.4 7.2 %collective-permute-start.8 = (f32[128]{0:T(128)S(1)}, f32[128]{0:T(128)S(1)}, u32[]{:S(2)}, u32[]{:S(2)}) collective-permute-start(f32[128]{0:T(128)S(1)} %get-tuple-element.70), channel_id=1, source_target_pairs={{0,2},{1,3},{2,4},{3,5},{4,6},{5,7},{6,8},{7,9},{8,10},{9,11},{10,... | collective-permute-start | bytes 1544 | tf_op jit(solution)/shard_map/ppermute | solution.py:27
  146.7 6.9 %collective-permute-start.9 = (f32[128]{0:T(128)S(1)}, f32[128]{0:T(128)S(1)}, u32[]{:S(2)}, u32[]{:S(2)}) collective-permute-start(f32[128]{0:T(128)S(1)} %get-tuple-element.69), channel_id=1, source_target_pairs={{0,3},{1,4},{2,5},{3,6},{4,7},{5,8},{6,9},{7,10},{8,11},{9,12},{10... | collective-permute-start | bytes 1544 | tf_op jit(solution)/shard_map/ppermute | solution.py:27
  290.1 1.0 copy-start.7
  303.0 16.5 %copy-start.8 = (f32[512,512]{1,0:T(8,128)S(1)}, f32[512,512]{1,0:T(8,128)}, u32[]{:S(2)}) copy-start(f32[512,512]{1,0:T(8,128)} %copy-done.7) | copy-start | bytes 3145732
  389.9 49.4 %copy-start.6 = (f32[512,512]{1,0:T(8,128)}, f32[512,512]{1,0:T(8,128)S(1)}, u32[]{:S(2)}) copy-start(f32[512,512]{1,0:T(8,128)S(1)} %get-tuple-element.139) | copy-start | bytes 3145732
  453.0 7.7 %copy-start.2 = (f32[2304,512]{1,0:T(8,128)S(1)}, f32[2304,512]{1,0:T(8,128)}, u32[]{:S(2)}) copy-start(f32[2304,512]{1,0:T(8,128)} %copy.65) | copy-start | bytes 14155780
  475.8 8.5 %copy-start.1 = (f32[32,128]{1,0:T(8,128)S(1)}, f32[32,128]{1,0:T(8,128)}, u32[]{:S(2)}) copy-start(f32[32,128]{1,0:T(8,128)} %param.21) | copy-start | bytes 49156
Sparse Core Ops, SparseCore 0:
  125.4 150.4 all-reduce.3
